TPU v7x, 32 devices: a whole 2x2x4 slice. The times are simulated.
32 devices in a mesh: gx: 16 (over z, x, core), gy: 2 (over y).
Axes of the slice: x: 2, y: 2, z: 4, core: 2. Of those that a mesh axis runs over, the one named last changes fastest.
Arguments:
- volume_field: float32 [3, 256, 32, 128], P(None, 'gx', 'gy'), may hold values from -6 to 6
- diag_blocks: float32 [3, 3, 256, 32, 128], P(None, None, 'gx', 'gy'), may hold values from -4 to 4
- face_weights: float32 [6, 2, 256, 32, 128], P(None, None, 'gx', 'gy'), may hold values from 0.3 to 3
- boundary_field: float32 [16, 2, 1536], P('gx', 'gy'), may hold values from -6 to 6
- self_term: float32 [16, 2, 1536], P('gx', 'gy'), may hold values from 0.5 to 2
- coupling: float32 [16, 2, 1536], P('gx', 'gy'), may hold values from 0.3 to 3
- owner_map: int32 [16, 2, 1536], P('gx', 'gy'), may hold values from 0 to 1535, as said below
- left_basis: bfloat16 [32, 16, 2, 1536], P('gy', 'gx'), may hold values from -1 to 1
- right_basis: bfloat16 [256, 16, 2, 1536], P('gx', None, 'gy'), may hold values from -0.0390625 to 0.0390625
Outputs:
- volume_out: float32 [3, 256, 32, 128], P(None, 'gx', 'gy')
- boundary_out: float32 [16, 2, 1536], P('gx', 'gy')
Inputs may be any that keep to these rules, and one draw needn't show every extreme that they name: `owner_map`: within each subdomain (p, q) the 1536 entries name every surface edge of that subdomain exactly once.
All inputs are finite; a program needn't handle non-finite values.
Results may differ from a plain program's by a relative error of at most 0.0017.
Values may be sent and summed in bfloat16 or wider, within the bound.
No kernel may reach another device: no remote copies, remote signals or barrier semaphores. Data moves between devices by JAX's collectives and lax.ppermute only.
A program may use at most 64 MiB of HBM per device.

v0:
```python
import jax
import jax.numpy as jnp
from jax import lax
from jax.sharding import PartitionSpec as P


def with_halo(value, sides, width):
    for axis, dim in sides:
        devices, length = (lax.axis_size(axis), value.shape[dim])
        up = [(i, (i + 1) % devices) for i in range(devices - 1)]
        down = [(j, i) for i, j in up]
        last = lax.slice_in_dim(value, length - width, length, axis=dim)
        initial = lax.slice_in_dim(value, 0, width, axis=dim)
        before = lax.ppermute(last, axis, up)
        after = lax.ppermute(initial, axis, down)
        value = jnp.concatenate([before, value, after], axis=dim)
    return value


def apply_blocks(field_in, diag_blocks, face_weights, neighbours):
    comp_rows = []
    for comp in range(3):
        accum_row = (
            diag_blocks[comp, 0] * field_in[0]
            + diag_blocks[comp, 1] * field_in[1]
            + diag_blocks[comp, 2] * field_in[2]
        )
        comp_rows.append(accum_row)
    for offset in range(6):
        direction = offset // 2
        tangent = [comp for comp in range(3) if comp != direction]
        for slot in range(2):
            comp_rows[tangent[slot]] = (
                comp_rows[tangent[slot]] - face_weights[offset, slot] * neighbours[offset][slot]
            )
    return jnp.stack(comp_rows)


def on_device(
    volume_field,
    diag_blocks,
    face_weights,
    boundary_field,
    self_term,
    coupling,
    owner_map,
    left_basis,
    right_basis,
):
    z_padded = jnp.pad(volume_field[0:2], ((0, 0), (0, 0), (0, 0), (1, 1)))
    plus_z = z_padded[..., 2:]
    minus_z = z_padded[..., :-2]
    padded = with_halo(volume_field, (("gx", 1), ("gy", 2)), 1)
    plus_x = padded[1:3, 2:, 1:-1]
    minus_x = padded[1:3, :-2, 1:-1]
    plus_y = padded[0::2, 1:-1, 2:]
    minus_y = padded[0::2, 1:-1, :-2]
    neighbours = [plus_x, minus_x, plus_y, minus_y, plus_z, minus_z]
    stiffness = apply_blocks(volume_field, diag_blocks, face_weights, neighbours)
    cells_x = volume_field.shape[1]
    cells_y = volume_field.shape[2]
    boundary_count = boundary_field.shape[2]
    surface = jnp.stack([volume_field[..., 0], volume_field[..., -1]]).reshape(boundary_count)
    owner_flat = owner_map.reshape(boundary_count)
    edge_trace = surface[owner_flat].reshape(boundary_field.shape)
    placed = (
        jnp.zeros((boundary_count,), jnp.float32)
        .at[owner_flat]
        .set((coupling * boundary_field).reshape(boundary_count))
    )
    placed = placed.reshape(2, 3, cells_x, cells_y)
    volume_out = stiffness.at[:, :, :, 0].add(placed[0]).at[:, :, :, -1].add(placed[1])
    boundary_half = boundary_field.astype(jnp.bfloat16)
    gathered = lax.all_gather(boundary_half, "gx", axis=0, tiled=True)
    coef = jnp.einsum("rxbk,xbk->r", right_basis, gathered, preferred_element_type=jnp.float32)
    coef_half = coef.astype(jnp.bfloat16)
    partial_value = jnp.einsum(
        "rabk,r->abk", left_basis, coef_half, preferred_element_type=jnp.float32
    )
    integral = lax.psum_scatter(partial_value, "gy", scatter_dimension=1, tiled=True)
    boundary_out = self_term * boundary_field + integral + coupling * edge_trace
    return (volume_out, boundary_out)


def solution(mesh):
    return jax.shard_map(
        on_device,
        mesh=mesh,
        in_specs=(
            P(None, "gx", "gy", None),
            P(None, None, "gx", "gy", None),
            P(None, None, "gx", "gy", None),
            P("gx", "gy", None),
            P("gx", "gy", None),
            P("gx", "gy", None),
            P("gx", "gy", None),
            P("gy", "gx", None, None),
            P("gx", None, "gy", None),
        ),
        out_specs=(P(None, "gx", "gy", None), P("gx", "gy", None)),
        check_vma=False,
    )
```

profile of v0, /device:TPU:0, one launch (start us, length us, event | category | flops | bytes accessed | tf_op | source)
XLA Modules:
  0.0 75.5 jit_solution(9150187020478586098)
XLA Ops:
  0.6 0.0 copy-start
  0.6 0.0 copy-start.5
  0.7 0.0 copy-start.4
  0.7 0.0 copy-start.8
  0.7 1.4 %fusion.40 = (f32[3,1,16,128]{3,2,1,0:T(8,128)}, f32[3,1,16,128]{3,2,1,0:T(8,128)}) fusion(f32[3,16,16,128]{3,2,1,0:T(8,128)} %param.13), kind=kLoop, calls=%fused_computation.77 | loop fusion | bytes 98304 | tf_op jit(solution)/shard_map/slice | solution.py:13
  2.1 3.0 %collective-permute-start = (f32[3,1,16,128]{3,2,1,0:T(8,128)}, f32[3,1,16,128]{3,2,1,0:T(8,128)}, u32[]{:S(2)}, u32[]{:S(2)}) collective-permute-start(f32[3,1,16,128]{3,2,1,0:T(8,128)} %get-tuple-element.42), channel_id=1, source_target_pairs={{0,2},{2,4},{4,6},{6,8},{8,10},{10,12},{12,14},{14,16},{16,18},{18... | collective-permute-start | bytes 73736 | tf_op jit(solution)/shard_map/ppermute | solution.py:14
  5.1 1.3 %collective-permute-start.1 = (f32[3,1,16,128]{3,2,1,0:T(8,128)}, f32[3,1,16,128]{3,2,1,0:T(8,128)}, u32[]{:S(2)}, u32[]{:S(2)}) collective-permute-start(f32[3,1,16,128]{3,2,1,0:T(8,128)} %get-tuple-element.41), channel_id=1, source_target_pairs={{2,0},{4,2},{6,4},{8,6},{10,8},{12,10},{14,12},{16,14},{18,16},{20... | collective-permute-start | bytes 73736 | tf_op jit(solution)/shard_map/ppermute | solution.py:15
  6.4 1.3 %fusion.39 = (f32[3,16,16,1]{3,2,1,0:T(8,128)S(1)}, f32[3,16,16,1]{3,2,1,0:T(8,128)S(1)}) fusion(f32[3,16,16,128]{3,2,1,0:T(8,128)} %param.13), kind=kLoop, calls=%fused_computation.76 | loop fusion | bytes 12288 | tf_op jit(solution)/shard_map/slice | solution.py:63
  7.7 0.3 copy.61
  8.0 0.4 copy.62
  8.4 0.1 reshape.175
  8.5 0.0 copy-done.5
  8.6 0.0 copy-done.4
  8.6 24.6 %all_gather.3 = bf16[16,1,1536]{2,1,0:T(2,128)(2,1)S(1)} all-gather(bf16[1,1,1536]{2,1,0:T(2,128)(2,1)S(1)} %convert_element_type.8), channel_id=1, replica_groups=mesh['gx'=16,'gy'=2] {'gx'}, dimensions={0}, use_global_device_ids=true | all-gather | bytes 52224 | tf_op jit(solution)/shard_map/all_gather | solution.py:74
  33.2 0.0 copy-done
  33.2 0.0 copy-done.8
  33.2 1.1 %fusion.4 = f32[1,2,1536]{2,0,1:T(1,128)S(1)} fusion(bf16[16,16,1536]{2,1,0:T(8,128)(2,1)S(1)} %bitcast.103, bf16[16,1,1536]{2,1,0:T(2,128)(2,1)S(1)} %all_gather.3, bf16[16,2,1536]{2,1,0:T(2,128)(2,1)S(1)} %bitcast.100), kind=kOutput, calls=%fused_computation.10 | convolution fusion | flops 884752 | bytes 946176 | tf_op jit(solution)/shard_map/rabk,r->abk/dot_general | solution.py:77
  34.4 8.1 %all-reduce.1 = f32[1,2,1536]{2,1,0:T(2,128)S(1)} all-reduce(f32[1,2,1536]{2,1,0:T(2,128)S(1)} %copy.58), channel_id=2, replica_groups=mesh['gx'=16,'gy'=2] {'gy'}, use_global_device_ids=true, to_apply=%region_1.2.clone | all-reduce | flops 3072 | bytes 24576
  42.5 0.0 copy-start.9
  42.5 0.0 copy-start.6
  42.5 0.0 copy-start.7
  42.5 0.0 copy-start.1
  42.5 0.0 copy-start.3
  42.5 8.4 %gather_fusion = f32[1536]{0:T(1024)S(1)} fusion(f32[1536]{0:T(1024)S(1)} %reshape.175, s32[2048]{0:T(1024)S(1)} %pad_clamp_fusion), kind=kCustom, calls=%fused_computation | custom fusion | bytes 18432 | tf_op jit(solution)/shard_map/gather | solution.py:65
  50.9 0.0 copy-start.2
  50.9 0.0 copy-done.9
  50.9 0.7 dynamic-slice.14
  51.6 0.0 copy-done.6
  51.6 0.0 copy-done.7
  51.6 1.3 %fusion.34 = (f32[1,1,1536]{2,1,0:T(1,128)}, f32[1536]{0:T(1024)S(1)}) fusion(f32[1,2,1536]{2,1,0:T(2,128)S(1)} %all-reduce.1, u32[]{:T(128)} %bitcast.32, f32[1,1,1536]{2,1,0:T(1,128)S(1)} %copy-done.6, f32[1536]{0:T(1024)S(1)} %gather_fusion, f32[1,1,1536]{2,1,0:T(1,128)S(1)} %copy-done.7, f32[1,1,1536]{2,1,0:T(1,128)S(1)} %copy-done.4), kind=kLoop, calls=%fused_computation.70 | loop fusion | flops 7680 | bytes 43012 | tf_op jit(solution)/shard_map/add | solution.py:81
  52.9 6.2 %scatter_custom_fusion = f32[1536]{0:T(1024)S(1)} fusion(s32[1536]{0:T(1024)S(1)} %fusion.33, f32[1536]{0:T(1024)S(1)} %get-tuple-element.48, f32[]{:T(128)} %constant.58.clone.1), kind=kCustom, calls=%fused_computation.72 | custom fusion | bytes 6148 | tf_op jit(solution)/shard_map/scatter | solution.py:69
  59.1 0.6 fusion.41
  59.7 0.0 copy-done.1
  59.7 0.1 reshape.170
  59.8 0.8 reshape.171
  60.5 0.0 collective-permute-done
  60.5 0.7 constant_dynamic-update-slice_fusion.6
  61.3 0.1 constant_dynamic-update-slice_fusion.4
  61.4 0.0 collective-permute-done.1
  61.4 0.7 constant_dynamic-update-slice_fusion.3
  62.2 2.4 %collective-permute-start.2 = (f32[3,18,1,128]{3,2,1,0:T(1,128)S(1)}, f32[3,18,1,128]{3,2,1,0:T(1,128)S(1)}, u32[]{:S(2)}, u32[]{:S(2)}) collective-permute-start(f32[3,18,1,128]{3,2,1,0:T(1,128)S(1)} %get-tuple-element.34), channel_id=1, source_target_pairs={{0,1},{2,3},{4,5},{6,7},{8,9},{10,11},{12,13},{14,15},{16,17},{18,... | collective-permute-start | bytes 82952 | tf_op jit(solution)/shard_map/ppermute | solution.py:14
  64.6 1.3 %collective-permute-start.3 = (f32[3,18,1,128]{3,2,1,0:T(1,128)S(1)}, f32[3,18,1,128]{3,2,1,0:T(1,128)S(1)}, u32[]{:S(2)}, u32[]{:S(2)}) collective-permute-start(f32[3,18,1,128]{3,2,1,0:T(1,128)S(1)} %get-tuple-element.35), channel_id=1, source_target_pairs={{1,0},{3,2},{5,4},{7,6},{9,8},{11,10},{13,12},{15,14},{17,16},{19,... | collective-permute-start | bytes 82952 | tf_op jit(solution)/shard_map/ppermute | solution.py:15
  65.9 0.0 copy-done.3
  65.9 0.0 copy-done.2
  65.9 0.2 fusion.12
  66.1 0.0 collective-permute-done.2
  66.1 4.2 %collective-permute-done.3 = f32[3,18,1,128]{3,2,1,0:T(1,128)S(1)} collective-permute-done((f32[3,18,1,128]{3,2,1,0:T(1,128)S(1)}, f32[3,18,1,128]{3,2,1,0:T(1,128)S(1)}, u32[]{:S(2)}, u32[]{:S(2)}) %collective-permute-start.3) | collective-permute-done | bytes 27680 | tf_op jit(solution)/shard_map/ppermute | solution.py:15
  70.4 0.1 pad_maximum_fusion
  70.5 0.2 fusion.8
  70.7 0.1 fusion.14
  70.8 0.8 %pad_maximum_fusion.1 = f32[3,16,16,128]{3,2,1,0:T(8,128)} fusion(f32[1,16,16,128]{3,2,1,0:T(8,128)S(1)} %fusion.14, f32[1,16,16,128]{3,2,1,0:T(8,128)S(1)} %fusion.12, f32[1,16,16,128]{3,2,1,0:T(8,128)S(1)} %fusion.8), kind=kLoop, calls=%fused_computation.12 | loop fusion | flops 196608 | bytes 786432 | tf_op jit(solution)/shard_map/stack | solution.py:36
  71.6 2.1 %copy.51 = f32[3,16,16,128]{2,1,0,3:T(8,128)S(1)} copy(f32[3,16,16,128]{3,2,1,0:T(8,128)} %pad_maximum_fusion.1) | data formatting | bytes 786432 | tf_op jit(solution)/shard_map/stack | solution.py:36
  73.7 1.8 %copy.54 = f32[3,16,16,128]{3,2,1,0:T(8,128)} copy(f32[3,16,16,128]{2,1,0,3:T(8,128)S(1)} %fusion.31) | data formatting | bytes 786432
  (10 shorter events, 0.2 us)
Async XLA Ops:
  0.6 32.6 %copy-start = (bf16[16,1,2,1536]{3,2,1,0:T(2,128)(2,1)S(1)}, bf16[16,1,2,1536]{3,2,1,0:T(2,128)(2,1)}, u32[]{:S(2)}) copy-start(bf16[16,1,2,1536]{3,2,1,0:T(2,128)(2,1)} %param.20) | copy-start | bytes 294916
  0.6 7.9 %copy-start.5 = (s32[1,1,1536]{2,1,0:T(1,128)S(1)}, s32[1,1,1536]{2,1,0:T(1,128)}, u32[]{:S(2)}) copy-start(s32[1,1,1536]{2,1,0:T(1,128)} %param.19) | copy-start | bytes 18436
  0.7 7.9 %copy-start.4 = (f32[1,1,1536]{2,1,0:T(1,128)S(1)}, f32[1,1,1536]{2,1,0:T(1,128)}, u32[]{:S(2)}) copy-start(f32[1,1,1536]{2,1,0:T(1,128)} %param.16) | copy-start | bytes 18436
  0.7 32.6 %copy-start.8 = (bf16[16,16,1,1536]{3,1,2,0:T(8,128)(2,1)S(1)}, bf16[16,16,1,1536]{3,1,2,0:T(8,128)(2,1)}, u32[]{:S(2)}) copy-start(bf16[16,16,1,1536]{3,1,2,0:T(8,128)(2,1)} %param.21) | copy-start | bytes 2359300
  2.1 58.4 %collective-permute-start = (f32[3,1,16,128]{3,2,1,0:T(8,128)}, f32[3,1,16,128]{3,2,1,0:T(8,128)}, u32[]{:S(2)}, u32[]{:S(2)}) collective-permute-start(f32[3,1,16,128]{3,2,1,0:T(8,128)} %get-tuple-element.42), channel_id=1, source_target_pairs={{0,2},{2,4},{4,6},{6,8},{8,10},{10,12},{12,14},{14,16},{16,18},{18... | collective-permute-start | bytes 73736 | tf_op jit(solution)/shard_map/ppermute | solution.py:14
  5.1 56.3 %collective-permute-start.1 = (f32[3,1,16,128]{3,2,1,0:T(8,128)}, f32[3,1,16,128]{3,2,1,0:T(8,128)}, u32[]{:S(2)}, u32[]{:S(2)}) collective-permute-start(f32[3,1,16,128]{3,2,1,0:T(8,128)} %get-tuple-element.41), channel_id=1, source_target_pairs={{2,0},{4,2},{6,4},{8,6},{10,8},{12,10},{14,12},{16,14},{18,16},{20... | collective-permute-start | bytes 73736 | tf_op jit(solution)/shard_map/ppermute | solution.py:15
  42.5 8.5 %copy-start.9 = (u32[32]{0:T(128)S(1)}, u32[32]{0:T(128)}, u32[]{:S(2)}) copy-start(u32[32]{0:T(128)} %constant.72) | copy-start | bytes 388
  42.5 9.1 %copy-start.6 = (f32[1,1,1536]{2,1,0:T(1,128)S(1)}, f32[1,1,1536]{2,1,0:T(1,128)}, u32[]{:S(2)}) copy-start(f32[1,1,1536]{2,1,0:T(1,128)} %param.18) | copy-start | bytes 18436
  42.5 9.1 %copy-start.7 = (f32[1,1,1536]{2,1,0:T(1,128)S(1)}, f32[1,1,1536]{2,1,0:T(1,128)}, u32[]{:S(2)}) copy-start(f32[1,1,1536]{2,1,0:T(1,128)} %param.17) | copy-start | bytes 18436
  42.5 17.2 %copy-start.1 = (f32[3,16,16,128]{3,2,1,0:T(8,128)S(1)}, f32[3,16,16,128]{3,2,1,0:T(8,128)}, u32[]{:S(2)}) copy-start(f32[3,16,16,128]{3,2,1,0:T(8,128)} %param.13) | copy-start | bytes 1179652
  42.5 23.4 %copy-start.3 = (f32[3,3,16,16,128]{4,3,2,1,0:T(8,128)S(1)}, f32[3,3,16,16,128]{4,3,2,1,0:T(8,128)}, u32[]{:S(2)}) copy-start(f32[3,3,16,16,128]{4,3,2,1,0:T(8,128)} %param.14) | copy-start | bytes 3538948
  50.9 15.0 %copy-start.2 = (f32[6,2,16,16,128]{4,3,2,1,0:T(8,128)S(1)}, f32[6,2,16,16,128]{4,3,2,1,0:T(8,128)}, u32[]{:S(2)}) copy-start(f32[6,2,16,16,128]{4,3,2,1,0:T(8,128)} %param.15) | copy-start | bytes 4718596
  62.2 4.0 %collective-permute-start.2 = (f32[3,18,1,128]{3,2,1,0:T(1,128)S(1)}, f32[3,18,1,128]{3,2,1,0:T(1,128)S(1)}, u32[]{:S(2)}, u32[]{:S(2)}) collective-permute-start(f32[3,18,1,128]{3,2,1,0:T(1,128)S(1)} %get-tuple-element.34), channel_id=1, source_target_pairs={{0,1},{2,3},{4,5},{6,7},{8,9},{10,11},{12,13},{14,15},{16,17},{18,... | collective-permute-start | bytes 82952 | tf_op jit(solution)/shard_map/ppermute | solution.py:14
  64.6 5.8 %collective-permute-start.3 = (f32[3,18,1,128]{3,2,1,0:T(1,128)S(1)}, f32[3,18,1,128]{3,2,1,0:T(1,128)S(1)}, u32[]{:S(2)}, u32[]{:S(2)}) collective-permute-start(f32[3,18,1,128]{3,2,1,0:T(1,128)S(1)} %get-tuple-element.35), channel_id=1, source_target_pairs={{1,0},{3,2},{5,4},{7,6},{9,8},{11,10},{13,12},{15,14},{17,16},{19,... | collective-permute-start | bytes 82952 | tf_op jit(solution)/shard_map/ppermute | solution.py:15
where the time goes:
time: 75.9 us; the launch traced here: 75.5 us
  blocking collectives  32.7 us (43%)
  local copies, waits for them, and re-layouts  25.7 us (34%)
  starting transfers between devices  7.98 us (11%)
  waiting for transfers between devices  4.27 us (6%)
  other arithmetic  2.72 us (4%)
  matrix products  1.12 us (1%)
  between operations  0.9 us (1%)
    all_gather x1, blocking collectives, on_device(): gathered = lax.all_gather(boundary_half, 'gx', axis=0, tiled=True)  24.6 us
    gather x1, local copies, waits for them, and re-layouts, on_device(): edge_trace = surface[owner_flat].reshape(boundary_field.shape)  8.39 us
    unnamed x1, blocking collectives  8.11 us
    scatter x1, local copies, waits for them, and re-layouts, on_device(): placed = jnp.zeros((boundary_count,), jnp.float32).at[owner_flat].set((co...  6.18 us
    ppermute x2, starting transfers between devices, with_halo(): before = lax.ppermute(last, axis, up)  5.41 us
    ppermute x2, waiting for transfers between devices, with_halo(): after = lax.ppermute(initial, axis, down)  4.23 us
    unnamed x26, local copies, waits for them, and re-layouts  4.02 us
    ppermute x2, starting transfers between devices, with_halo(): after = lax.ppermute(initial, axis, down)  2.57 us
  transfers between devices with their start and end apart: 4, of which 1 were waited for; matrix products, arithmetic and copies ran while one was open for 29% of the time, Pallas kernels for 0%

commit v1 on v0

--- a/solution.py
+++ b/solution.py
@@ -71,8 +71,26 @@
     placed = placed.reshape(2, 3, cells_x, cells_y)
     volume_out = stiffness.at[:, :, :, 0].add(placed[0]).at[:, :, :, -1].add(placed[1])
     boundary_half = boundary_field.astype(jnp.bfloat16)
-    gathered = lax.all_gather(boundary_half, "gx", axis=0, tiled=True)
-    coef = jnp.einsum("rxbk,xbk->r", right_basis, gathered, preferred_element_type=jnp.float32)
+    devices_2, here = (lax.axis_size("gx"), lax.axis_index("gx"))
+    behind = [(i_2, (i_2 - 1) % devices_2) for i_2 in range(devices_2)]
+    rows = boundary_half.shape[0]
+    current = boundary_half
+    coef = jnp.einsum(
+        "rxbk,xbk->r",
+        lax.dynamic_slice_in_dim(right_basis, here * rows, current.shape[0], axis=1),
+        current,
+        preferred_element_type=jnp.float32,
+    )
+    for step in range(1, devices_2):
+        current = lax.ppermute(current, "gx", behind)
+        coef = coef + jnp.einsum(
+            "rxbk,xbk->r",
+            lax.dynamic_slice_in_dim(
+                right_basis, (here + step) % devices_2 * rows, current.shape[0], axis=1
+            ),
+            current,
+            preferred_element_type=jnp.float32,
+        )
     coef_half = coef.astype(jnp.bfloat16)
     partial_value = jnp.einsum(
         "rabk,r->abk", left_basis, coef_half, preferred_element_type=jnp.float32

time: 75.9 us -> 139 us (1.83)
  starting transfers between devices: 7.98 us -> 69 us
  blocking collectives: 32.7 us -> 9.8 us
  matrix products: 1.12 us -> 9.3 us
  waiting for transfers between devices: 4.27 us -> 10.7 us
  local copies, waits for them, and re-layouts: 25.7 us -> 31.6 us
  other arithmetic: 2.72 us -> 6.75 us
    ppermute x0 -> x15, starting transfers between devices: none -> 60.5 us  [on_device(): current = lax.ppermute(current, 'gx', behind)]
    all_gather x1 -> x0, blocking collectives: 24.6 us -> none  [on_device(): gathered = lax.all_gather(boundary_half, 'gx', axis=0, tiled=True)]
    ppermute x0 -> x15, waiting for transfers between devices: none -> 10.7 us  [on_device(): current = lax.ppermute(current, 'gx', behind)]
    dot_general x0 -> x15, matrix products: none -> 8.15 us  [the longest x14 8.03 us: on_device(): jnp.einsum('rxbk,xbk->r', lax.dynamic_slice_in_dim(right_basis, (here + s...]
    ppermute x2, waiting for transfers between devices: 4.23 us -> 0.01 us  [with_halo(): after = lax.ppermute(initial, axis, down)]
    dynamic_slice x0 -> x1, local copies, waits for them, and re-layouts: none -> 2.7 us  [on_device(): lax.dynamic_slice_in_dim(right_basis, (here + step) % devices_2 * rows, c...]
    slice x1, local copies, waits for them, and re-layouts: 0.04 us -> 1.85 us  [with_halo(): last = lax.slice_in_dim(value, length - width, length, axis=dim)]
    unnamed x1, blocking collectives: 8.11 us -> 9.8 us
  transfers between devices with their start and end apart: 4 -> 19, of which waited for: 1 -> 13; matrix products, arithmetic and copies ran while one was open for 29% -> 29% of each run, Pallas kernels for 0% -> 0%
where the time goes in v1:
time: 139 us; the launch traced here: 138 us
  starting transfers between devices  69 us (50%)
  local copies, waits for them, and re-layouts  31.6 us (23%)
  waiting for transfers between devices  10.7 us (8%)
  blocking collectives  9.8 us (7%)
  matrix products  9.3 us (7%)
  other arithmetic  6.75 us (5%)
    ppermute x15, starting transfers between devices, on_device(): current = lax.ppermute(current, 'gx', behind)  60.5 us
    ppermute x15, waiting for transfers between devices, on_device(): current = lax.ppermute(current, 'gx', behind)  10.7 us
    unnamed x1, blocking collectives  9.8 us
    gather x1, local copies, waits for them, and re-layouts, on_device(): edge_trace = surface[owner_flat].reshape(boundary_field.shape)  8.39 us
    dot_general x14, matrix products, on_device(): jnp.einsum('rxbk,xbk->r', lax.dynamic_slice_in_dim(right_basis, (here + s...  8.03 us
    scatter x1, local copies, waits for them, and re-layouts, on_device(): placed = jnp.zeros((boundary_count,), jnp.float32).at[owner_flat].set((co...  6.18 us
    ppermute x2, starting transfers between devices, with_halo(): before = lax.ppermute(last, axis, up)  5.91 us
    unnamed x46, local copies, waits for them, and re-layouts  5.31 us
  transfers between devices with their start and end apart: 19, of which 13 were waited for; matrix products, arithmetic and copies ran while one was open for 29% of the time, Pallas kernels for 0%

profile of v1, /device:TPU:0, one launch (start us, length us, event | category | flops | bytes accessed | tf_op | source)
XLA Modules:
  0.0 138.4 jit_solution(5151179981781235638)
XLA Ops:
  0.7 0.8 convert_element_type.8
  1.4 5.4 %collective-permute-start.4 = (bf16[1,1,1536]{2,1,0:T(2,128)(2,1)S(1)}, bf16[1,1,1536]{2,1,0:T(2,128)(2,1)}, u32[]{:S(2)}, u32[]{:S(2)}) collective-permute-start(bf16[1,1,1536]{2,1,0:T(2,128)(2,1)S(1)} %convert_element_type.8), channel_id=1, source_target_pairs={{0,30},{2,0},{4,2},{6,4},{8,6},{10,8},{12,10},{14,12},{16,14},{18,... | collective-permute-start | bytes 9224 | tf_op jit(solution)/shard_map/ppermute | solution.py:85
  6.9 1.4 fusion.68
  8.3 1.9 %collective-permute-start = (f32[3,1,16,128]{3,2,1,0:T(8,128)}, f32[3,1,16,128]{3,2,1,0:T(8,128)}, u32[]{:S(2)}, u32[]{:S(2)}) collective-permute-start(f32[3,1,16,128]{3,2,1,0:T(8,128)} %get-tuple-element.56), channel_id=1, source_target_pairs={{0,2},{2,4},{4,6},{6,8},{8,10},{10,12},{12,14},{14,16},{16,18},{18... | collective-permute-start | bytes 73736 | tf_op jit(solution)/shard_map/ppermute | solution.py:14
  10.2 1.3 collective-permute-start.1
  11.6 1.3 fusion.67
  13.0 2.7 %constant_dynamic-slice_fusion = (bf16[16,1,1,1536]{3,1,2,0:T(2,128)(2,1)}, bf16[16,1,1,1536]{3,1,2,0:T(2,128)(2,1)}, bf16[16,1,1,1536]{3,1,2,0:T(2,128)(2,1)}, ...) fusion(bf16[16,16,1,1536]{3,1,2,0:T(8,128)(2,1)S(1)} %copy-done, ...), kind=kLoop, calls=%fused_computation.132 | loop fusion | bytes 1572928 | tf_op jit(solution)/shard_map/dynamic_slice | solution.py:88
  15.9 0.3 copy.102
  16.2 0.4 copy.103
  16.8 8.4 %gather_fusion = f32[1536]{0:T(1024)S(1)} fusion(f32[1536]{0:T(1024)S(1)} %reshape.295, s32[2048]{0:T(1024)S(1)} %pad_clamp_fusion), kind=kCustom, calls=%fused_computation | custom fusion | bytes 18432 | tf_op jit(solution)/shard_map/gather | solution.py:65
  25.2 0.6 dynamic-slice.14
  25.8 2.2 %collective-permute-start.5 = (bf16[1,1,1536]{2,1,0:T(2,128)(2,1)}, bf16[1,1,1536]{2,1,0:T(2,128)(2,1)S(1)}, u32[]{:S(2)}, u32[]{:S(2)}) collective-permute-start(bf16[1,1,1536]{2,1,0:T(2,128)(2,1)} %collective-permute-done.4), channel_id=1, source_target_pairs={{0,30},{2,0},{4,2},{6,4},{8,6},{10,8},{12,10},{14,12},{16,14},{18,... | collective-permute-start | bytes 9224 | tf_op jit(solution)/shard_map/ppermute | solution.py:85
  28.0 1.0 fusion
  29.0 0.5 collective-permute-done.5
  29.5 4.4 %collective-permute-start.6 = (bf16[1,1,1536]{2,1,0:T(2,128)(2,1)S(1)}, bf16[1,1,1536]{2,1,0:T(2,128)(2,1)S(1)}, u32[]{:S(2)}, u32[]{:S(2)}) collective-permute-start(bf16[1,1,1536]{2,1,0:T(2,128)(2,1)S(1)} %collective-permute-done.5), channel_id=1, source_target_pairs={{0,30},{2,0},{4,2},{6,4},{8,6},{10,8},{12,10},{14,12},{16,14},{18,... | collective-permute-start | bytes 9224 | tf_op jit(solution)/shard_map/ppermute | solution.py:85
  34.0 1.0 fusion.1
  35.0 0.3 collective-permute-done.6
  35.3 4.4 %collective-permute-start.7 = (bf16[1,1,1536]{2,1,0:T(2,128)(2,1)S(1)}, bf16[1,1,1536]{2,1,0:T(2,128)(2,1)S(1)}, u32[]{:S(2)}, u32[]{:S(2)}) collective-permute-start(bf16[1,1,1536]{2,1,0:T(2,128)(2,1)S(1)} %collective-permute-done.6), channel_id=1, source_target_pairs={{0,30},{2,0},{4,2},{6,4},{8,6},{10,8},{12,10},{14,12},{16,14},{18,... | collective-permute-start | bytes 9224 | tf_op jit(solution)/shard_map/ppermute | solution.py:85
  39.7 1.0 fusion.2
  40.7 0.3 collective-permute-done.7
  41.1 4.4 %collective-permute-start.8 = (bf16[1,1,1536]{2,1,0:T(2,128)(2,1)S(1)}, bf16[1,1,1536]{2,1,0:T(2,128)(2,1)S(1)}, u32[]{:S(2)}, u32[]{:S(2)}) collective-permute-start(bf16[1,1,1536]{2,1,0:T(2,128)(2,1)S(1)} %collective-permute-done.7), channel_id=1, source_target_pairs={{0,30},{2,0},{4,2},{6,4},{8,6},{10,8},{12,10},{14,12},{16,14},{18,... | collective-permute-start | bytes 9224 | tf_op jit(solution)/shard_map/ppermute | solution.py:85
  45.5 1.0 fusion.3
  46.5 0.3 collective-permute-done.8
  46.8 4.4 %collective-permute-start.9 = (bf16[1,1,1536]{2,1,0:T(2,128)(2,1)S(1)}, bf16[1,1,1536]{2,1,0:T(2,128)(2,1)S(1)}, u32[]{:S(2)}, u32[]{:S(2)}) collective-permute-start(bf16[1,1,1536]{2,1,0:T(2,128)(2,1)S(1)} %collective-permute-done.8), channel_id=1, source_target_pairs={{0,30},{2,0},{4,2},{6,4},{8,6},{10,8},{12,10},{14,12},{16,14},{18,... | collective-permute-start | bytes 9224 | tf_op jit(solution)/shard_map/ppermute | solution.py:85
  51.2 1.0 fusion.4
  52.2 0.3 collective-permute-done.9
  52.6 4.4 %collective-permute-start.10 = (bf16[1,1,1536]{2,1,0:T(2,128)(2,1)S(1)}, bf16[1,1,1536]{2,1,0:T(2,128)(2,1)S(1)}, u32[]{:S(2)}, u32[]{:S(2)}) collective-permute-start(bf16[1,1,1536]{2,1,0:T(2,128)(2,1)S(1)} %collective-permute-done.9), channel_id=1, source_target_pairs={{0,30},{2,0},{4,2},{6,4},{8,6},{10,8},{12,10},{14,12},{16,14},{18,... | collective-permute-start | bytes 9224 | tf_op jit(solution)/shard_map/ppermute | solution.py:85
  57.0 1.0 fusion.5
  58.0 0.3 collective-permute-done.10
  58.3 4.4 %collective-permute-start.11 = (bf16[1,1,1536]{2,1,0:T(2,128)(2,1)S(1)}, bf16[1,1,1536]{2,1,0:T(2,128)(2,1)S(1)}, u32[]{:S(2)}, u32[]{:S(2)}) collective-permute-start(bf16[1,1,1536]{2,1,0:T(2,128)(2,1)S(1)} %collective-permute-done.10), channel_id=1, source_target_pairs={{0,30},{2,0},{4,2},{6,4},{8,6},{10,8},{12,10},{14,12},{16,14},{18,... | collective-permute-start | bytes 9224 | tf_op jit(solution)/shard_map/ppermute | solution.py:85
  62.7 1.0 fusion.6
  63.7 1.4 constant_dynamic-update-slice_fusion.6
  65.1 0.8 constant_dynamic-update-slice_fusion.4
  66.0 1.6 %constant_dynamic-update-slice_fusion.3 = (f32[3,17,16,128]{3,2,1,0:T(8,128)S(1)}, f32[3,18,16,128]{3,2,1,0:T(8,128)}) fusion(f32[3,17,16,128]{3,2,1,0:T(8,128)S(1)} %get-tuple-element.52, f32[3,1,16,128]{3,2,1,0:T(8,128)} %collective-permute-done.1, f32[3,18,16,128]{3,2,1,0:T(8,128)} %get-tuple-element.53), kind=kLoop, calls=%fused_computation.107 | loop fusion | bytes 73728 | tf_op jit(solution)/shard_map/concatenate | solution.py:16
  67.5 1.8 %fusion.66 = (f32[3,18,1,128]{3,2,1,0:T(1,128)}, f32[3,18,1,128]{3,2,1,0:T(1,128)}) fusion(f32[3,18,16,128]{3,2,1,0:T(8,128)} %get-tuple-element.58), kind=kLoop, calls=%fused_computation.152 | loop fusion | bytes 110592 | tf_op jit(solution)/shard_map/slice | solution.py:12
  69.4 4.0 %collective-permute-start.2 = (f32[3,18,1,128]{3,2,1,0:T(1,128)}, f32[3,18,1,128]{3,2,1,0:T(1,128)}, u32[]{:S(2)}, u32[]{:S(2)}) collective-permute-start(f32[3,18,1,128]{3,2,1,0:T(1,128)} %get-tuple-element.48), channel_id=1, source_target_pairs={{0,1},{2,3},{4,5},{6,7},{8,9},{10,11},{12,13},{14,15},{16,17},{18,... | collective-permute-start | bytes 82952 | tf_op jit(solution)/shard_map/ppermute | solution.py:14
  73.4 1.3 collective-permute-start.3
  74.7 0.8 fusion.24
  75.5 0.1 fusion.7
  75.7 1.2 collective-permute-done.12
  76.9 4.4 %collective-permute-start.13 = (bf16[1,1,1536]{2,1,0:T(2,128)(2,1)S(1)}, bf16[1,1,1536]{2,1,0:T(2,128)(2,1)S(1)}, u32[]{:S(2)}, u32[]{:S(2)}) collective-permute-start(bf16[1,1,1536]{2,1,0:T(2,128)(2,1)S(1)} %collective-permute-done.12), channel_id=1, source_target_pairs={{0,30},{2,0},{4,2},{6,4},{8,6},{10,8},{12,10},{14,12},{16,14},{18,... | collective-permute-start | bytes 9224 | tf_op jit(solution)/shard_map/ppermute | solution.py:85
  81.4 1.2 collective-permute-done.13
  82.6 4.4 %collective-permute-start.14 = (bf16[1,1,1536]{2,1,0:T(2,128)(2,1)S(1)}, bf16[1,1,1536]{2,1,0:T(2,128)(2,1)S(1)}, u32[]{:S(2)}, u32[]{:S(2)}) collective-permute-start(bf16[1,1,1536]{2,1,0:T(2,128)(2,1)S(1)} %collective-permute-done.13), channel_id=1, source_target_pairs={{0,30},{2,0},{4,2},{6,4},{8,6},{10,8},{12,10},{14,12},{16,14},{18,... | collective-permute-start | bytes 9224 | tf_op jit(solution)/shard_map/ppermute | solution.py:85
  87.2 1.2 collective-permute-done.14
  88.4 4.4 %collective-permute-start.15 = (bf16[1,1,1536]{2,1,0:T(2,128)(2,1)S(1)}, bf16[1,1,1536]{2,1,0:T(2,128)(2,1)S(1)}, u32[]{:S(2)}, u32[]{:S(2)}) collective-permute-start(bf16[1,1,1536]{2,1,0:T(2,128)(2,1)S(1)} %collective-permute-done.14), channel_id=1, source_target_pairs={{0,30},{2,0},{4,2},{6,4},{8,6},{10,8},{12,10},{14,12},{16,14},{18,... | collective-permute-start | bytes 9224 | tf_op jit(solution)/shard_map/ppermute | solution.py:85
  92.9 1.2 collective-permute-done.15
  94.1 4.4 %collective-permute-start.16 = (bf16[1,1,1536]{2,1,0:T(2,128)(2,1)S(1)}, bf16[1,1,1536]{2,1,0:T(2,128)(2,1)S(1)}, u32[]{:S(2)}, u32[]{:S(2)}) collective-permute-start(bf16[1,1,1536]{2,1,0:T(2,128)(2,1)S(1)} %collective-permute-done.15), channel_id=1, source_target_pairs={{0,30},{2,0},{4,2},{6,4},{8,6},{10,8},{12,10},{14,12},{16,14},{18,... | collective-permute-start | bytes 9224 | tf_op jit(solution)/shard_map/ppermute | solution.py:85
  98.5 0.1 fusion.11
  98.7 1.2 collective-permute-done.16
  99.9 4.4 %collective-permute-start.17 = (bf16[1,1,1536]{2,1,0:T(2,128)(2,1)S(1)}, bf16[1,1,1536]{2,1,0:T(2,128)(2,1)S(1)}, u32[]{:S(2)}, u32[]{:S(2)}) collective-permute-start(bf16[1,1,1536]{2,1,0:T(2,128)(2,1)S(1)} %collective-permute-done.16), channel_id=1, source_target_pairs={{0,30},{2,0},{4,2},{6,4},{8,6},{10,8},{12,10},{14,12},{16,14},{18,... | collective-permute-start | bytes 9224 | tf_op jit(solution)/shard_map/ppermute | solution.py:85
  104.4 1.2 collective-permute-done.17
  105.6 4.4 %collective-permute-start.18 = (bf16[1,1,1536]{2,1,0:T(2,128)(2,1)S(1)}, bf16[1,1,1536]{2,1,0:T(2,128)(2,1)S(1)}, u32[]{:S(2)}, u32[]{:S(2)}) collective-permute-start(bf16[1,1,1536]{2,1,0:T(2,128)(2,1)S(1)} %collective-permute-done.17), channel_id=1, source_target_pairs={{0,30},{2,0},{4,2},{6,4},{8,6},{10,8},{12,10},{14,12},{16,14},{18,... | collective-permute-start | bytes 9224 | tf_op jit(solution)/shard_map/ppermute | solution.py:85
  110.2 1.2 collective-permute-done.18
  111.4 1.1 fusion.17
  112.6 9.8 %all-reduce.1 = f32[1,2,1536]{2,1,0:T(2,128)S(1)} all-reduce(f32[1,2,1536]{2,1,0:T(2,128)S(1)} %copy.83), channel_id=2, replica_groups=mesh['gx'=16,'gy'=2] {'gy'}, use_global_device_ids=true, to_apply=%region_1.2.clone | all-reduce | flops 3072 | bytes 24576
  122.4 1.9 %fusion.61 = (f32[1,1,1536]{2,1,0:T(1,128)}, f32[1536]{0:T(1024)S(1)}) fusion(f32[1,2,1536]{2,1,0:T(2,128)S(1)} %all-reduce.1, u32[]{:T(128)} %bitcast.77, f32[1,1,1536]{2,1,0:T(1,128)} %param.18, f32[1536]{0:T(1024)S(1)} %gather_fusion, f32[1,1,1536]{2,1,0:T(1,128)} %param.17, f32[1,1,1536]{2,1,0:T(1,128)S(1)} %copy-done.17), kind=kLoop, calls=%fused_computation.130 | loop fusion | flops 7680 | bytes 43012 | tf_op jit(solution)/shard_map/add | solution.py:99
  124.2 6.2 %scatter_custom_fusion = f32[1536]{0:T(1024)S(1)} fusion(s32[1536]{0:T(1024)S(1)} %fusion.43, f32[1536]{0:T(1024)S(1)} %get-tuple-element.62, f32[]{:T(128)} %constant.143.clone.1), kind=kCustom, calls=%fused_computation.148 | custom fusion | bytes 6148 | tf_op jit(solution)/shard_map/scatter | solution.py:69
  130.5 0.7 reshape.261
  131.2 1.1 pad_maximum_fusion
  132.4 1.1 fusion.26
  133.5 0.2 fusion.20
  133.7 0.8 pad_maximum_fusion.1
  134.5 2.1 %copy.62 = f32[3,16,16,128]{2,1,0,3:T(8,128)S(1)} copy(f32[3,16,16,128]{3,2,1,0:T(8,128)} %pad_maximum_fusion.1) | data formatting | bytes 786432 | tf_op jit(solution)/shard_map/stack | solution.py:36
  136.6 1.8 %copy.81 = f32[3,16,16,128]{3,2,1,0:T(8,128)} copy(f32[3,16,16,128]{2,1,0,3:T(8,128)S(1)} %fusion.41) | data formatting | bytes 786432
  (64 shorter events, 1.2 us)
Async XLA Ops:
  0.6 110.8 %copy-start = (bf16[16,1,2,1536]{3,2,1,0:T(2,128)(2,1)S(1)}, bf16[16,1,2,1536]{3,2,1,0:T(2,128)(2,1)}, u32[]{:S(2)}) copy-start(bf16[16,1,2,1536]{3,2,1,0:T(2,128)(2,1)} %param.20) | copy-start | bytes 294916
  0.6 12.3 %copy-start.2 = (bf16[16,16,1,1536]{3,1,2,0:T(8,128)(2,1)S(1)}, bf16[16,16,1,1536]{3,1,2,0:T(8,128)(2,1)}, u32[]{:S(2)}) copy-start(bf16[16,16,1,1536]{3,1,2,0:T(8,128)(2,1)} %param.21) | copy-start | bytes 2359300
  1.4 24.3 %collective-permute-start.4 = (bf16[1,1,1536]{2,1,0:T(2,128)(2,1)S(1)}, bf16[1,1,1536]{2,1,0:T(2,128)(2,1)}, u32[]{:S(2)}, u32[]{:S(2)}) collective-permute-start(bf16[1,1,1536]{2,1,0:T(2,128)(2,1)S(1)} %convert_element_type.8), channel_id=1, source_target_pairs={{0,30},{2,0},{4,2},{6,4},{8,6},{10,8},{12,10},{14,12},{16,14},{18,... | collective-permute-start | bytes 9224 | tf_op jit(solution)/shard_map/ppermute | solution.py:85
  8.3 55.5 %collective-permute-start = (f32[3,1,16,128]{3,2,1,0:T(8,128)}, f32[3,1,16,128]{3,2,1,0:T(8,128)}, u32[]{:S(2)}, u32[]{:S(2)}) collective-permute-start(f32[3,1,16,128]{3,2,1,0:T(8,128)} %get-tuple-element.56), channel_id=1, source_target_pairs={{0,2},{2,4},{4,6},{6,8},{8,10},{10,12},{12,14},{14,16},{16,18},{18... | collective-permute-start | bytes 73736 | tf_op jit(solution)/shard_map/ppermute | solution.py:14
  10.2 55.8 %collective-permute-start.1 = (f32[3,1,16,128]{3,2,1,0:T(8,128)}, f32[3,1,16,128]{3,2,1,0:T(8,128)}, u32[]{:S(2)}, u32[]{:S(2)}) collective-permute-start(f32[3,1,16,128]{3,2,1,0:T(8,128)} %get-tuple-element.55), channel_id=1, source_target_pairs={{2,0},{4,2},{6,4},{8,6},{10,8},{12,10},{14,12},{16,14},{18,16},{20... | collective-permute-start | bytes 73736 | tf_op jit(solution)/shard_map/ppermute | solution.py:15
  13.0 2.7 %copy-start.16 = (f32[1,1,1536]{2,1,0:T(1,128)S(1)}, f32[1,1,1536]{2,1,0:T(1,128)}, u32[]{:S(2)}) copy-start(f32[1,1,1536]{2,1,0:T(1,128)} %param.16) | copy-start | bytes 18436
  13.0 3.5 %copy-start.18 = (s32[1,1,1536]{2,1,0:T(1,128)S(1)}, s32[1,1,1536]{2,1,0:T(1,128)}, u32[]{:S(2)}) copy-start(s32[1,1,1536]{2,1,0:T(1,128)} %param.19) | copy-start | bytes 18436
  13.0 3.6 %copy-start.1 = (f32[3,16,16,128]{3,2,1,0:T(8,128)S(1)}, f32[3,16,16,128]{3,2,1,0:T(8,128)}, u32[]{:S(2)}) copy-start(f32[3,16,16,128]{3,2,1,0:T(8,128)} %param.13) | copy-start | bytes 1179652
  16.8 8.4 %copy-start.19 = (u32[32]{0:T(128)S(1)}, u32[32]{0:T(128)}, u32[]{:S(2)}) copy-start(u32[32]{0:T(128)} %constant.175) | copy-start | bytes 388
  16.8 57.9 %copy-start.4 = (f32[3,3,16,16,128]{4,3,2,1,0:T(8,128)S(1)}, f32[3,3,16,16,128]{4,3,2,1,0:T(8,128)}, u32[]{:S(2)}) copy-start(f32[3,3,16,16,128]{4,3,2,1,0:T(8,128)} %param.14) | copy-start | bytes 3538948
  25.2 49.5 %copy-start.3 = (f32[6,2,16,16,128]{4,3,2,1,0:T(8,128)S(1)}, f32[6,2,16,16,128]{4,3,2,1,0:T(8,128)}, u32[]{:S(2)}) copy-start(f32[6,2,16,16,128]{4,3,2,1,0:T(8,128)} %param.15) | copy-start | bytes 4718596
  25.8 3.8 %collective-permute-start.5 = (bf16[1,1,1536]{2,1,0:T(2,128)(2,1)}, bf16[1,1,1536]{2,1,0:T(2,128)(2,1)S(1)}, u32[]{:S(2)}, u32[]{:S(2)}) collective-permute-start(bf16[1,1,1536]{2,1,0:T(2,128)(2,1)} %collective-permute-done.4), channel_id=1, source_target_pairs={{0,30},{2,0},{4,2},{6,4},{8,6},{10,8},{12,10},{14,12},{16,14},{18,... | collective-permute-start | bytes 9224 | tf_op jit(solution)/shard_map/ppermute | solution.py:85
  29.5 5.8 %collective-permute-start.6 = (bf16[1,1,1536]{2,1,0:T(2,128)(2,1)S(1)}, bf16[1,1,1536]{2,1,0:T(2,128)(2,1)S(1)}, u32[]{:S(2)}, u32[]{:S(2)}) collective-permute-start(bf16[1,1,1536]{2,1,0:T(2,128)(2,1)S(1)} %collective-permute-done.5), channel_id=1, source_target_pairs={{0,30},{2,0},{4,2},{6,4},{8,6},{10,8},{12,10},{14,12},{16,14},{18,... | collective-permute-start | bytes 9224 | tf_op jit(solution)/shard_map/ppermute | solution.py:85
  35.3 5.8 %collective-permute-start.7 = (bf16[1,1,1536]{2,1,0:T(2,128)(2,1)S(1)}, bf16[1,1,1536]{2,1,0:T(2,128)(2,1)S(1)}, u32[]{:S(2)}, u32[]{:S(2)}) collective-permute-start(bf16[1,1,1536]{2,1,0:T(2,128)(2,1)S(1)} %collective-permute-done.6), channel_id=1, source_target_pairs={{0,30},{2,0},{4,2},{6,4},{8,6},{10,8},{12,10},{14,12},{16,14},{18,... | collective-permute-start | bytes 9224 | tf_op jit(solution)/shard_map/ppermute | solution.py:85
  41.1 5.8 %collective-permute-start.8 = (bf16[1,1,1536]{2,1,0:T(2,128)(2,1)S(1)}, bf16[1,1,1536]{2,1,0:T(2,128)(2,1)S(1)}, u32[]{:S(2)}, u32[]{:S(2)}) collective-permute-start(bf16[1,1,1536]{2,1,0:T(2,128)(2,1)S(1)} %collective-permute-done.7), channel_id=1, source_target_pairs={{0,30},{2,0},{4,2},{6,4},{8,6},{10,8},{12,10},{14,12},{16,14},{18,... | collective-permute-start | bytes 9224 | tf_op jit(solution)/shard_map/ppermute | solution.py:85
  46.8 5.8 %collective-permute-start.9 = (bf16[1,1,1536]{2,1,0:T(2,128)(2,1)S(1)}, bf16[1,1,1536]{2,1,0:T(2,128)(2,1)S(1)}, u32[]{:S(2)}, u32[]{:S(2)}) collective-permute-start(bf16[1,1,1536]{2,1,0:T(2,128)(2,1)S(1)} %collective-permute-done.8), channel_id=1, source_target_pairs={{0,30},{2,0},{4,2},{6,4},{8,6},{10,8},{12,10},{14,12},{16,14},{18,... | collective-permute-start | bytes 9224 | tf_op jit(solution)/shard_map/ppermute | solution.py:85
  52.6 5.8 %collective-permute-start.10 = (bf16[1,1,1536]{2,1,0:T(2,128)(2,1)S(1)}, bf16[1,1,1536]{2,1,0:T(2,128)(2,1)S(1)}, u32[]{:S(2)}, u32[]{:S(2)}) collective-permute-start(bf16[1,1,1536]{2,1,0:T(2,128)(2,1)S(1)} %collective-permute-done.9), channel_id=1, source_target_pairs={{0,30},{2,0},{4,2},{6,4},{8,6},{10,8},{12,10},{14,12},{16,14},{18,... | collective-permute-start | bytes 9224 | tf_op jit(solution)/shard_map/ppermute | solution.py:85
  58.3 17.2 %collective-permute-start.11 = (bf16[1,1,1536]{2,1,0:T(2,128)(2,1)S(1)}, bf16[1,1,1536]{2,1,0:T(2,128)(2,1)S(1)}, u32[]{:S(2)}, u32[]{:S(2)}) collective-permute-start(bf16[1,1,1536]{2,1,0:T(2,128)(2,1)S(1)} %collective-permute-done.10), channel_id=1, source_target_pairs={{0,30},{2,0},{4,2},{6,4},{8,6},{10,8},{12,10},{14,12},{16,14},{18,... | collective-permute-start | bytes 9224 | tf_op jit(solution)/shard_map/ppermute | solution.py:85
  65.1 10.4 %copy-start.14 = (bf16[16,1,1,1536]{3,1,2,0:T(2,128)(2,1)S(1)}, bf16[16,1,1,1536]{3,1,2,0:T(2,128)(2,1)}, u32[]{:S(2)}) copy-start(bf16[16,1,1,1536]{3,1,2,0:T(2,128)(2,1)} %get-tuple-element.37) | copy-start | bytes 147460
  65.1 16.2 %copy-start.13 = (bf16[16,1,1,1536]{3,1,2,0:T(2,128)(2,1)S(1)}, bf16[16,1,1,1536]{3,1,2,0:T(2,128)(2,1)}, u32[]{:S(2)}) copy-start(bf16[16,1,1,1536]{3,1,2,0:T(2,128)(2,1)} %get-tuple-element.36) | copy-start | bytes 147460
  65.1 21.9 %copy-start.12 = (bf16[16,1,1,1536]{3,1,2,0:T(2,128)(2,1)S(1)}, bf16[16,1,1,1536]{3,1,2,0:T(2,128)(2,1)}, u32[]{:S(2)}) copy-start(bf16[16,1,1,1536]{3,1,2,0:T(2,128)(2,1)} %get-tuple-element.35) | copy-start | bytes 147460
  65.9 9.6 %copy-start.7 = (f32[3,17,16,128]{3,2,1,0:T(8,128)}, f32[3,17,16,128]{3,2,1,0:T(8,128)S(1)}, u32[]{:S(2)}) copy-start(f32[3,17,16,128]{3,2,1,0:T(8,128)S(1)} %get-tuple-element.54) | copy-start | bytes 1253380
  65.9 26.9 %copy-start.11 = (bf16[16,1,1,1536]{3,1,2,0:T(2,128)(2,1)S(1)}, bf16[16,1,1,1536]{3,1,2,0:T(2,128)(2,1)}, u32[]{:S(2)}) copy-start(bf16[16,1,1,1536]{3,1,2,0:T(2,128)(2,1)} %get-tuple-element.34) | copy-start | bytes 147460
  65.9 32.6 %copy-start.10 = (bf16[16,1,1,1536]{3,1,2,0:T(2,128)(2,1)S(1)}, bf16[16,1,1,1536]{3,1,2,0:T(2,128)(2,1)}, u32[]{:S(2)}) copy-start(bf16[16,1,1,1536]{3,1,2,0:T(2,128)(2,1)} %get-tuple-element.33) | copy-start | bytes 147460
  65.9 38.4 %copy-start.9 = (bf16[16,1,1,1536]{3,1,2,0:T(2,128)(2,1)S(1)}, bf16[16,1,1,1536]{3,1,2,0:T(2,128)(2,1)}, u32[]{:S(2)}) copy-start(bf16[16,1,1,1536]{3,1,2,0:T(2,128)(2,1)} %get-tuple-element.32) | copy-start | bytes 147460
  65.9 44.1 %copy-start.8 = (bf16[16,1,1,1536]{3,1,2,0:T(2,128)(2,1)S(1)}, bf16[16,1,1,1536]{3,1,2,0:T(2,128)(2,1)}, u32[]{:S(2)}) copy-start(bf16[16,1,1,1536]{3,1,2,0:T(2,128)(2,1)} %get-tuple-element.31) | copy-start | bytes 147460
  65.9 56.4 %copy-start.17 = (f32[1,1,1536]{2,1,0:T(1,128)S(1)}, f32[1,1,1536]{2,1,0:T(1,128)}, u32[]{:S(2)}) copy-start(f32[1,1,1536]{2,1,0:T(1,128)} %param.16) | copy-start | bytes 18436
  67.5 7.2 %copy-start.5 = (f32[3,17,16,128]{3,2,1,0:T(8,128)}, f32[3,17,16,128]{3,2,1,0:T(8,128)S(1)}, u32[]{:S(2)}) copy-start(f32[3,17,16,128]{3,2,1,0:T(8,128)S(1)} %get-tuple-element.57) | copy-start | bytes 1253380
  69.4 61.8 %collective-permute-start.2 = (f32[3,18,1,128]{3,2,1,0:T(1,128)}, f32[3,18,1,128]{3,2,1,0:T(1,128)}, u32[]{:S(2)}, u32[]{:S(2)}) collective-permute-start(f32[3,18,1,128]{3,2,1,0:T(1,128)} %get-tuple-element.48), channel_id=1, source_target_pairs={{0,1},{2,3},{4,5},{6,7},{8,9},{10,11},{12,13},{14,15},{16,17},{18,... | collective-permute-start | bytes 82952 | tf_op jit(solution)/shard_map/ppermute | solution.py:14
  73.4 57.8 %collective-permute-start.3 = (f32[3,18,1,128]{3,2,1,0:T(1,128)}, f32[3,18,1,128]{3,2,1,0:T(1,128)}, u32[]{:S(2)}, u32[]{:S(2)}) collective-permute-start(f32[3,18,1,128]{3,2,1,0:T(1,128)} %get-tuple-element.49), channel_id=1, source_target_pairs={{1,0},{3,2},{5,4},{7,6},{9,8},{11,10},{13,12},{15,14},{17,16},{19,... | collective-permute-start | bytes 82952 | tf_op jit(solution)/shard_map/ppermute | solution.py:15
  75.5 1.4 collective-permute-start.12
  76.9 5.8 %collective-permute-start.13 = (bf16[1,1,1536]{2,1,0:T(2,128)(2,1)S(1)}, bf16[1,1,1536]{2,1,0:T(2,128)(2,1)S(1)}, u32[]{:S(2)}, u32[]{:S(2)}) collective-permute-start(bf16[1,1,1536]{2,1,0:T(2,128)(2,1)S(1)} %collective-permute-done.12), channel_id=1, source_target_pairs={{0,30},{2,0},{4,2},{6,4},{8,6},{10,8},{12,10},{14,12},{16,14},{18,... | collective-permute-start | bytes 9224 | tf_op jit(solution)/shard_map/ppermute | solution.py:85
  82.6 5.8 %collective-permute-start.14 = (bf16[1,1,1536]{2,1,0:T(2,128)(2,1)S(1)}, bf16[1,1,1536]{2,1,0:T(2,128)(2,1)S(1)}, u32[]{:S(2)}, u32[]{:S(2)}) collective-permute-start(bf16[1,1,1536]{2,1,0:T(2,128)(2,1)S(1)} %collective-permute-done.13), channel_id=1, source_target_pairs={{0,30},{2,0},{4,2},{6,4},{8,6},{10,8},{12,10},{14,12},{16,14},{18,... | collective-permute-start | bytes 9224 | tf_op jit(solution)/shard_map/ppermute | solution.py:85
  88.4 5.8 %collective-permute-start.15 = (bf16[1,1,1536]{2,1,0:T(2,128)(2,1)S(1)}, bf16[1,1,1536]{2,1,0:T(2,128)(2,1)S(1)}, u32[]{:S(2)}, u32[]{:S(2)}) collective-permute-start(bf16[1,1,1536]{2,1,0:T(2,128)(2,1)S(1)} %collective-permute-done.14), channel_id=1, source_target_pairs={{0,30},{2,0},{4,2},{6,4},{8,6},{10,8},{12,10},{14,12},{16,14},{18,... | collective-permute-start | bytes 9224 | tf_op jit(solution)/shard_map/ppermute | solution.py:85
  94.1 5.8 %collective-permute-start.16 = (bf16[1,1,1536]{2,1,0:T(2,128)(2,1)S(1)}, bf16[1,1,1536]{2,1,0:T(2,128)(2,1)S(1)}, u32[]{:S(2)}, u32[]{:S(2)}) collective-permute-start(bf16[1,1,1536]{2,1,0:T(2,128)(2,1)S(1)} %collective-permute-done.15), channel_id=1, source_target_pairs={{0,30},{2,0},{4,2},{6,4},{8,6},{10,8},{12,10},{14,12},{16,14},{18,... | collective-permute-start | bytes 9224 | tf_op jit(solution)/shard_map/ppermute | solution.py:85
  99.9 5.8 %collective-permute-start.17 = (bf16[1,1,1536]{2,1,0:T(2,128)(2,1)S(1)}, bf16[1,1,1536]{2,1,0:T(2,128)(2,1)S(1)}, u32[]{:S(2)}, u32[]{:S(2)}) collective-permute-start(bf16[1,1,1536]{2,1,0:T(2,128)(2,1)S(1)} %collective-permute-done.16), channel_id=1, source_target_pairs={{0,30},{2,0},{4,2},{6,4},{8,6},{10,8},{12,10},{14,12},{16,14},{18,... | collective-permute-start | bytes 9224 | tf_op jit(solution)/shard_map/ppermute | solution.py:85
  105.6 5.8 %collective-permute-start.18 = (bf16[1,1,1536]{2,1,0:T(2,128)(2,1)S(1)}, bf16[1,1,1536]{2,1,0:T(2,128)(2,1)S(1)}, u32[]{:S(2)}, u32[]{:S(2)}) collective-permute-start(bf16[1,1,1536]{2,1,0:T(2,128)(2,1)S(1)} %collective-permute-done.17), channel_id=1, source_target_pairs={{0,30},{2,0},{4,2},{6,4},{8,6},{10,8},{12,10},{14,12},{16,14},{18,... | collective-permute-start | bytes 9224 | tf_op jit(solution)/shard_map/ppermute | solution.py:85
  132.4 1.3 copy-start.6
  134.5 2.1 %copy-start.15 = (f32[3,16,16,1]{2,1,0,3:T(8,128)S(1)}, f32[3,16,16,1]{2,1,0,3:T(8,128)}, u32[]{:S(2)}) copy-start(f32[3,16,16,1]{2,1,0,3:T(8,128)} %reshape.261) | copy-start | bytes 9220
